TPU v7x, 32 devices: a whole 2x2x4 slice. The times are simulated.
32 devices in a mesh: groups: 2 (over y), wide: 4 (over z), narrow: 4 (over x, core).
Axes of the slice: x: 2, y: 2, z: 4, core: 2. Of those that a mesh axis runs over, the one named last changes fastest.
Arguments:
- generator: int32 [8192], P('narrow'), may hold values from 1 to 511
- lattice_shift: int32 [16384], P(('groups', 'narrow')), parts along dimension 0, may hold values from 0 to 1023
- loadings: bfloat16 [512, 4, 64, 128], P(('groups', 'wide')), parts along dimension 0, may hold values from -0.375 to 0.375
- load_pattern: int32 [512, 4], P(('groups', 'wide')), parts along dimension 0, may hold values from 0 to 127
- threshold: float32 [65536], P(('groups', 'wide')), parts along dimension 0, may hold values from -2.5 to -0.5
- exposure: float32 [65536], P(('groups', 'wide')), parts along dimension 0, may hold values from 0.1 to 2
- segment_map: int32 [65536], P(('groups', 'wide')), parts along dimension 0, may hold values from 0 to 4095, as said below
- net_tiles: bfloat16 [64, 8, 128, 128], P(('groups', 'wide')), parts along dimension 0, may hold values from -0.1875 to 0.1875
- net_pattern: int32 [64, 8], P(('groups', 'wide')), parts along dimension 0, may hold values from 0 to 7
Outputs:
- net_loss: float32 [512, 8192], P('narrow', ('groups', 'wide')), parts along dimension 1
- moments: float32 [2, 8192], P(None, ('groups', 'wide')), parts along dimension 1
There are 2 independent parts, one for each index of `groups`. A program takes and returns all parts, laid end to end along the dimension named above; an argument that names none is the same for every part. Nothing has to cross between parts.
Inputs may be any that keep to these rules, and one draw needn't show every extreme that they name: `segment_map`: in each aligned block of 8192 obligors at most 3072 map to the same group of 1024 consecutive segments; one group receives exactly 3072 obligors from every block.
All inputs are finite; a program needn't handle non-finite values.
Results may differ from a plain program's by a relative error of at most 0.0036.
Values may be sent and summed in bfloat16 or wider, within the bound.
No kernel may reach another device: no remote copies, remote signals or barrier semaphores. Data moves between devices by JAX's collectives and lax.ppermute only.
A program may use at most 64 MiB of HBM per device.

v0:
```python
import jax
import jax.numpy as jnp
from jax import lax
from jax.sharding import PartitionSpec as P

P_SIZE = 512
SEG_DEV = 1024


def normal_cdf(values):
    return 0.5 * lax.erfc(-values * 0.7071067811865476)


def normal_quantile(values):
    return 1.4142135623730951 * lax.erf_inv(2.0 * values - 1.0)


def normal_points(count, generator, lattice_shift):
    points = jnp.arange(count, dtype=jnp.int32)
    residue = points[:, None] * generator[None, :] % P_SIZE
    offset = (lattice_shift.astype(jnp.float32) + 0.5) / 1024.0
    uniform = (residue.astype(jnp.float32) + offset[None, :]) / P_SIZE
    return normal_quantile(uniform).astype(jnp.bfloat16)


def body(
    generator,
    lattice_shift,
    loadings,
    load_pattern,
    threshold,
    exposure,
    segment_map,
    net_tiles,
    net_pattern,
):
    narrow_size = lax.axis_size("narrow")
    local_points = P_SIZE // narrow_size
    panel = normal_points(P_SIZE, generator, lattice_shift)
    factors = lax.all_to_all(panel, "narrow", split_axis=0, concat_axis=1, tiled=True)
    factor_width = factors.shape[1]
    factor_tiles = factors.T.reshape(factor_width // 64, 64, local_points)
    picked = factor_tiles[load_pattern]
    latent = jnp.einsum("bkfp,bkfi->pbi", picked, loadings, preferred_element_type=jnp.float32)
    latent = latent.reshape(local_points, -1)
    default_prob = normal_cdf(threshold[None, :] - latent)
    weighted = (exposure[None, :] * default_prob).astype(jnp.bfloat16)
    by_row = weighted.T
    groups = lax.axis_size("wide")
    partial_sums = jax.ops.segment_sum(
        by_row.astype(jnp.float32), segment_map, num_segments=groups * SEG_DEV
    )
    seg_loss = lax.psum_scatter(partial_sums, "wide", scatter_dimension=0, tiled=True)
    loss_blocks = seg_loss.astype(jnp.bfloat16).reshape(-1, 128, local_points)
    gathered = loss_blocks[net_pattern]
    netted = jnp.einsum("bkjp,bkji->pbi", gathered, net_tiles, preferred_element_type=jnp.float32)
    netted = netted.reshape(local_points, -1)
    first_sum, second_sum = lax.psum(
        (jnp.sum(netted, axis=0), jnp.sum(netted * netted, axis=0)), "narrow"
    )
    moments = jnp.stack([first_sum, second_sum]) / P_SIZE
    return (netted, moments)


def solution(mesh):
    return jax.shard_map(
        body,
        mesh=mesh,
        in_specs=(
            P("narrow"),
            P(("groups", "narrow")),
            P(("groups", "wide"), None, None, None),
            P(("groups", "wide"), None),
            P(("groups", "wide")),
            P(("groups", "wide")),
            P(("groups", "wide")),
            P(("groups", "wide"), None, None, None),
            P(("groups", "wide"), None),
        ),
        out_specs=(P("narrow", ("groups", "wide")), P(None, ("groups", "wide"))),
        check_vma=False,
    )
```

profile of v0, /device:TPU:0, one launch (start us, length us, event | category | flops | bytes accessed | tf_op | source)
XLA Modules:
  0.0 184.4 jit_solution(4201307887410369890)
XLA Ops:
  7.2 0.0 copy-start
  7.2 0.0 copy-start.4
  7.2 0.0 copy-start.2
  7.2 0.8 add_multiply_fusion
  8.1 12.4 %multiply_convert_fusion = bf16[4,128,2048]{1,2,0:T(8,128)(2,1)} fusion(f32[2048]{0:T(1024)S(1)} %add_multiply_fusion, s32[2048]{0:T(1024)} %param.9, s32[4,128]{1,0:T(4,128)S(1)} %multiply_add_fusion), kind=kLoop, calls=%fused_computation.38 | loop fusion | flops 57671680 | bytes 2115584 | tf_op jit(solution)/shard_map/convert_element_type | solution.py:23
  20.4 4.4 %all-to-all-start = ((bf16[4,128,2048]{1,2,0:T(8,128)(2,1)}), bf16[4,128,2048]{1,2,0:T(8,128)(2,1)}, u32[]{:S(2)}, u32[]{:S(2)}) async-start(bf16[4,128,2048]{1,2,0:T(8,128)(2,1)} %multiply_convert_fusion), calls=%async_computation | async-start | bytes 4194304 | tf_op jit(solution)/shard_map/all_to_all | solution.py:40
  24.9 0.0 reduce-scatter.2.cloned.1.call-start
  24.9 0.0 copy-done.4
  25.0 0.1 copy.13
  25.1 0.1 reshape.52
  25.2 0.0 copy-done.2
  25.2 26.1 %all-to-all-done = bf16[4,128,2048]{1,2,0:T(8,128)(2,1)} async-done(((bf16[4,128,2048]{1,2,0:T(8,128)(2,1)}), bf16[4,128,2048]{1,2,0:T(8,128)(2,1)}, u32[]{:S(2)}, u32[]{:S(2)}) %all-to-all-start) | async-done | bytes 2097184 | tf_op jit(solution)/shard_map/all_to_all | solution.py:40
  51.3 4.6 %gather_fusion = bf16[256,64,128]{2,1,0:T(8,128)(2,1)} fusion(bf16[128,64,128]{2,1,0:T(8,128)(2,1)} %bitcast.3, s32[1024]{0:T(1024)S(1)} %pad_clamp_fusion.1), kind=kCustom, calls=%fused_computation | custom fusion | bytes 8389632 | tf_op jit(solution)/shard_map/gather | solution.py:43
  55.9 0.0 copy-start.1
  55.9 4.8 %fusion.24 = f32[64,128,128,1]{1,2,3,0:T(8,128)S(1)} fusion(bf16[64,4,64,128]{3,2,1,0:T(8,128)(2,1)} %bitcast.43, bf16[64,4,64,128]{3,2,1,0:T(8,128)(2,1)} %param.11), kind=kOutput, calls=%fused_computation.54 | convolution fusion | flops 536870912 | bytes 12582912 | tf_op jit(solution)/shard_map/bkfp,bkfi->pbi/dot_general | solution.py:44
  60.7 0.0 copy-done.1
  60.7 11.9 %fusion.8 = bf16[128,8192]{0,1:T(8,128)(2,1)} fusion(f32[64,128,128,1]{1,2,3,0:T(8,128)S(1)} %fusion.24, f32[8192]{0:T(1024)S(1)} %broadcast_multiply_fusion, f32[8192]{0:T(1024)S(1)} %copy-done.1), kind=kLoop, calls=%fused_computation.18 | loop fusion | flops 68157440 | bytes 6356992 | tf_op jit(solution)/shard_map/convert_element_type | solution.py:47
  72.6 0.0 copy-start.3
  72.6 46.0 %scatter_custom_fusion = f32[4096,128]{1,0:T(8,128)} fusion(s32[8192]{0:T(1024)} %param.15, bf16[128,8192]{0,1:T(8,128)(2,1)} %fusion.8, f32[]{:T(128)} %constant.62.clone.1), kind=kCustom, calls=%fused_computation.23 | custom fusion | flops 2097152 | bytes 4194816 | tf_op jit(solution)/shard_map/scatter-add | solution.py:50
  118.5 0.0 reduce-scatter.2.cloned.1.call-update
  118.6 0.0 copy-done.3
  118.6 0.1 reshape.60
  118.7 45.0 %reduce-scatter.2.cloned.1.call-done = f32[1024,128]{1,0:T(8,128)} async-done(((f32[4096,128]{1,0:T(8,128)}), f32[1024,128]{1,0:T(8,128)}) %reduce-scatter.2.cloned.1.call-update) | async-done | bytes 524304 | tf_op jit(solution)/shard_map/reduce_scatter | solution.py:53
  163.7 1.1 convert_element_type.29
  164.8 2.2 %gather_fusion.1 = bf16[64,128,128]{2,1,0:T(8,128)(2,1)} fusion(bf16[8,128,128]{2,1,0:T(8,128)(2,1)S(1)} %bitcast.42, s32[1024]{0:T(1024)S(1)} %pad_clamp_fusion), kind=kCustom, calls=%fused_computation.1 | custom fusion | bytes 4194560 | tf_op jit(solution)/shard_map/gather | solution.py:55
  167.0 0.0 copy-done
  167.0 2.5 %bitcast_reduce_fusion = (f32[8,128]{1,0:T(8,128)S(1)}, f32[8,128]{1,0:T(8,128)S(1)}, f32[8,128,128,1]{1,2,3,0:T(8,128)S(1)}) fusion(bf16[8,8,128,128]{3,2,1,0:T(8,128)(2,1)} %bitcast.44, bf16[8,8,128,128]{3,2,1,0:T(8,128)(2,1)S(1)} %copy-done), kind=kOutput, calls=%fused_computation.43 | convolution fusion | flops 268826624 | bytes 4726784 | tf_op jit(solution)/shard_map/bkjp,bkji->pbi/dot_general | solution.py:56
  169.5 1.0 copy.15
  170.5 6.5 %all-reduce = (f32[1,1024]{1,0:T(1,128)S(1)}, f32[1,1024]{1,0:T(1,128)S(1)}) all-reduce(f32[1,1024]{1,0:T(1,128)S(1)} %bitcast.47, f32[1,1024]{1,0:T(1,128)S(1)} %bitcast.46), channel_id=1, replica_groups=mesh['groups'=2,'wide'=4,'narrow'=4] {'narrow'}, use_global_device_ids=true, to_apply=%region_5.6 | all-reduce | flops 2048 | bytes 16384 | tf_op jit(solution)/shard_map/psum | solution.py:58
  177.0 0.6 maximum_multiply_fusion
  (6 shorter events, 0.0 us)
Async XLA Ops:
  7.2 159.8 %copy-start = (bf16[8,8,128,128]{3,2,1,0:T(8,128)(2,1)S(1)}, bf16[8,8,128,128]{3,2,1,0:T(8,128)(2,1)}, u32[]{:S(2)}) copy-start(bf16[8,8,128,128]{3,2,1,0:T(8,128)(2,1)} %param.16) | copy-start | bytes 6291460
  7.2 17.8 %copy-start.4 = (s32[64,4]{0,1:T(4,128)S(1)}, s32[64,4]{0,1:T(4,128)}, u32[]{:S(2)}) copy-start(s32[64,4]{0,1:T(4,128)} %param.12) | copy-start | bytes 3076
  7.2 18.0 %copy-start.2 = (f32[8192]{0:T(1024)S(1)}, f32[8192]{0:T(1024)}, u32[]{:S(2)}) copy-start(f32[8192]{0:T(1024)} %param.14) | copy-start | bytes 98308
  20.4 30.8 %all-to-all-start = ((bf16[4,128,2048]{1,2,0:T(8,128)(2,1)}), bf16[4,128,2048]{1,2,0:T(8,128)(2,1)}, u32[]{:S(2)}, u32[]{:S(2)}) async-start(bf16[4,128,2048]{1,2,0:T(8,128)(2,1)} %multiply_convert_fusion), calls=%async_computation | async-start | bytes 4194304 | tf_op jit(solution)/shard_map/all_to_all | solution.py:40
  24.9 138.8 %reduce-scatter.2.cloned.1.call-start = ((), (), s32[]{:S(2)}) async-start(), calls=%async_computation.2 | async-start | bytes 2621440 | tf_op jit(solution)/shard_map/reduce_scatter | solution.py:53
  55.9 4.8 %copy-start.1 = (f32[8192]{0:T(1024)S(1)}, f32[8192]{0:T(1024)}, u32[]{:S(2)}) copy-start(f32[8192]{0:T(1024)} %param.13) | copy-start | bytes 98308
  72.6 46.0 %copy-start.3 = (s32[8,8]{1,0:T(8,128)S(1)}, s32[8,8]{1,0:T(8,128)}, u32[]{:S(2)}) copy-start(s32[8,8]{1,0:T(8,128)} %param.17) | copy-start | bytes 772
Sparse Core Ops, SparseCore 0:
  118.7 44.9 reduce-scatter.1
where the time goes:
time: 185 us; the launch traced here: 184 us
  other arithmetic  72.8 us (39%)
  waiting for transfers between devices  71.1 us (38%)
  between operations  14.2 us (8%)
  local copies, waits for them, and re-layouts  8.08 us (4%)
  matrix products  7.29 us (4%)
  blocking collectives  6.49 us (4%)
  starting transfers between devices  4.48 us (2%)
    scatter-add x1, other arithmetic, body(): jax.ops.segment_sum(by_row.astype(jnp.float32), segment_map, num_segments...  46 us
    reduce_scatter x1, waiting for transfers between devices, body(): lax.psum_scatter(partial_sums, 'wide', scatter_dimension=0, tiled=True)  45 us
    all_to_all x1, waiting for transfers between devices, body(): lax.all_to_all(panel, 'narrow', split_axis=0, concat_axis=1, tiled=True)  26.1 us
    convert_element_type x1, other arithmetic, normal_points(): return normal_quantile(uniform).astype(jnp.bfloat16)  12.4 us
    convert_element_type x1, other arithmetic, body(): weighted = (exposure[None, :] * default_prob).astype(jnp.bfloat16)  11.9 us
    psum x1, blocking collectives, body(): lax.psum((jnp.sum(netted, axis=0), jnp.sum(netted * netted, axis=0)), 'na...  6.49 us
    dot_general x1, matrix products, body(): jnp.einsum('bkfp,bkfi->pbi', picked, loadings, preferred_element_type=jnp...  4.77 us
    gather x1, local copies, waits for them, and re-layouts, body(): picked = factor_tiles[load_pattern]  4.61 us
  transfers between devices with their start and end apart: 2, of which 2 were waited for; matrix products, arithmetic and copies ran while one was open for 0% of the time, Pallas kernels for 0%

commit v1 on v0

--- a/solution.py
+++ b/solution.py
@@ -37,7 +37,10 @@
     narrow_size = lax.axis_size("narrow")
     local_points = P_SIZE // narrow_size
     panel = normal_points(P_SIZE, generator, lattice_shift)
-    factors = lax.all_to_all(panel, "narrow", split_axis=0, concat_axis=1, tiled=True)
+    n_dev = lax.axis_size("narrow")
+    shards = jnp.stack(jnp.split(panel, n_dev, axis=0), axis=0)
+    shards = lax.all_to_all(shards, "narrow", split_axis=0, concat_axis=0)
+    factors = jnp.concatenate(shards, axis=1)
     factor_width = factors.shape[1]
     factor_tiles = factors.T.reshape(factor_width // 64, 64, local_points)
     picked = factor_tiles[load_pattern]

time: 185 us -> 186 us (level)
  no operation moved by 1% of the time
where the time goes in v1:
time: 186 us
  other arithmetic  73.6 us (40%)
  waiting for transfers between devices  71.2 us (38%)
  between operations  14.2 us (8%)
  local copies, waits for them, and re-layouts  8.45 us (5%)
  matrix products  7.28 us (4%)
  blocking collectives  6.47 us (3%)
  starting transfers between devices  4.48 us (2%)
    scatter-add x1, other arithmetic, body(): jax.ops.segment_sum(by_row.astype(jnp.float32), segment_map, num_segments...  46 us
    reduce_scatter x1, waiting for transfers between devices, body(): lax.psum_scatter(partial_sums, 'wide', scatter_dimension=0, tiled=True)  45.1 us
    all_to_all x1, waiting for transfers between devices, body(): shards = lax.all_to_all(shards, 'narrow', split_axis=0, concat_axis=0)  26.1 us
    convert_element_type x1, other arithmetic, body(): weighted = (exposure[None, :] * default_prob).astype(jnp.bfloat16)  11.9 us
    convert_element_type x1, other arithmetic, normal_points(): return normal_quantile(uniform).astype(jnp.bfloat16)  11.6 us
    psum x1, blocking collectives, body(): lax.psum((jnp.sum(netted, axis=0), jnp.sum(netted * netted, axis=0)), 'na...  6.47 us
    dot_general x1, matrix products, body(): jnp.einsum('bkfp,bkfi->pbi', picked, loadings, preferred_element_type=jnp...  4.76 us
    gather x1, local copies, waits for them, and re-layouts, body(): picked = factor_tiles[load_pattern]  4.61 us
  transfers between devices with their start and end apart: 2, of which 2 were waited for; matrix products, arithmetic and copies ran while one was open for 0% of the time, Pallas kernels for 0%

profile of v1, /device:TPU:0, one launch (start us, length us, event | category | flops | bytes accessed | tf_op | source)
XLA Modules:
  0.0 185.7 jit_solution(17928653216072321599)
XLA Ops:
  7.2 0.0 copy-start
  7.2 0.8 add_multiply_fusion
  8.0 11.6 %multiply_convert_fusion = bf16[512,2048]{0,1:T(8,128)(2,1)S(1)} fusion(f32[2048]{0:T(1024)S(1)} %add_multiply_fusion, s32[2048]{0:T(1024)} %param.9), kind=kLoop, calls=%fused_computation.36 | loop fusion | flops 57671680 | bytes 2113536 | tf_op jit(solution)/shard_map/convert_element_type | solution.py:23
  19.6 0.4 slice_bitcast_fusion.3
  20.0 0.0 copy-start.4
  20.0 0.0 copy-start.2
  20.0 1.6 pad_maximum_fusion
  21.6 4.4 %all-to-all-start = ((bf16[4,128,2048]{1,2,0:T(8,128)(2,1)}), bf16[4,128,2048]{1,2,0:T(8,128)(2,1)}, u32[]{:S(2)}, u32[]{:S(2)}) async-start(bf16[4,128,2048]{1,2,0:T(8,128)(2,1)} %pad_maximum_fusion), calls=%async_computation | async-start | bytes 4194304 | tf_op jit(solution)/shard_map/all_to_all | solution.py:42
  26.1 0.0 reduce-scatter.2.cloned.1.call-start
  26.1 0.0 copy-done.4
  26.2 0.1 copy.13
  26.3 0.1 reshape.38
  26.4 0.0 copy-done.2
  26.4 26.1 %all-to-all-done = bf16[4,128,2048]{1,2,0:T(8,128)(2,1)} async-done(((bf16[4,128,2048]{1,2,0:T(8,128)(2,1)}), bf16[4,128,2048]{1,2,0:T(8,128)(2,1)}, u32[]{:S(2)}, u32[]{:S(2)}) %all-to-all-start) | async-done | bytes 2097184 | tf_op jit(solution)/shard_map/all_to_all | solution.py:42
  52.5 4.6 %gather_fusion = bf16[256,64,128]{2,1,0:T(8,128)(2,1)} fusion(bf16[128,64,128]{2,1,0:T(8,128)(2,1)} %bitcast.7, s32[1024]{0:T(1024)S(1)} %pad_clamp_fusion.1), kind=kCustom, calls=%fused_computation | custom fusion | bytes 8389632 | tf_op jit(solution)/shard_map/gather | solution.py:46
  57.1 0.0 copy-start.1
  57.1 4.8 %fusion.27 = f32[64,128,128,1]{1,2,3,0:T(8,128)S(1)} fusion(bf16[64,4,64,128]{3,2,1,0:T(8,128)(2,1)} %bitcast.51, bf16[64,4,64,128]{3,2,1,0:T(8,128)(2,1)} %param.11), kind=kOutput, calls=%fused_computation.59 | convolution fusion | flops 536870912 | bytes 12582912 | tf_op jit(solution)/shard_map/bkfp,bkfi->pbi/dot_general | solution.py:47
  61.9 0.0 copy-done.1
  61.9 11.9 %fusion.9 = bf16[128,8192]{0,1:T(8,128)(2,1)} fusion(f32[64,128,128,1]{1,2,3,0:T(8,128)S(1)} %fusion.27, f32[8192]{0:T(1024)S(1)} %broadcast_multiply_fusion, f32[8192]{0:T(1024)S(1)} %copy-done.1), kind=kLoop, calls=%fused_computation.17 | loop fusion | flops 68157440 | bytes 6356992 | tf_op jit(solution)/shard_map/convert_element_type | solution.py:50
  73.8 0.0 copy-start.3
  73.8 46.0 %scatter_custom_fusion = f32[4096,128]{1,0:T(8,128)} fusion(s32[8192]{0:T(1024)} %param.15, bf16[128,8192]{0,1:T(8,128)(2,1)} %fusion.9, f32[]{:T(128)} %constant.62.clone.1), kind=kCustom, calls=%fused_computation.21 | custom fusion | flops 2097152 | bytes 4194816 | tf_op jit(solution)/shard_map/scatter-add | solution.py:53
  119.8 0.0 reduce-scatter.2.cloned.1.call-update
  119.8 0.0 copy-done.3
  119.8 0.1 reshape.46
  119.9 45.1 %reduce-scatter.2.cloned.1.call-done = f32[1024,128]{1,0:T(8,128)} async-done(((f32[4096,128]{1,0:T(8,128)}), f32[1024,128]{1,0:T(8,128)}) %reduce-scatter.2.cloned.1.call-update) | async-done | bytes 524304 | tf_op jit(solution)/shard_map/reduce_scatter | solution.py:56
  165.0 1.1 convert_element_type.27
  166.0 2.2 %gather_fusion.1 = bf16[64,128,128]{2,1,0:T(8,128)(2,1)} fusion(bf16[8,128,128]{2,1,0:T(8,128)(2,1)S(1)} %bitcast.50, s32[1024]{0:T(1024)S(1)} %pad_clamp_fusion), kind=kCustom, calls=%fused_computation.1 | custom fusion | bytes 4194560 | tf_op jit(solution)/shard_map/gather | solution.py:58
  168.2 0.0 copy-done
  168.2 2.5 %bitcast_reduce_fusion = (f32[8,128]{1,0:T(8,128)S(1)}, f32[8,128]{1,0:T(8,128)S(1)}, f32[8,128,128,1]{1,2,3,0:T(8,128)S(1)}) fusion(bf16[8,8,128,128]{3,2,1,0:T(8,128)(2,1)} %bitcast.52, bf16[8,8,128,128]{3,2,1,0:T(8,128)(2,1)S(1)} %copy-done), kind=kOutput, calls=%fused_computation.49 | convolution fusion | flops 268826624 | bytes 4726784 | tf_op jit(solution)/shard_map/bkjp,bkji->pbi/dot_general | solution.py:59
  170.7 1.0 copy.15
  171.7 6.5 %all-reduce = (f32[1,1024]{1,0:T(1,128)S(1)}, f32[1,1024]{1,0:T(1,128)S(1)}) all-reduce(f32[1,1024]{1,0:T(1,128)S(1)} %bitcast.55, f32[1,1024]{1,0:T(1,128)S(1)} %bitcast.54), channel_id=1, replica_groups=mesh['groups'=2,'wide'=4,'narrow'=4] {'narrow'}, use_global_device_ids=true, to_apply=%region_5.6 | all-reduce | flops 2048 | bytes 16384 | tf_op jit(solution)/shard_map/psum | solution.py:61
  178.2 0.6 maximum_multiply_fusion
  (5 shorter events, 0.0 us)
Async XLA Ops:
  7.2 161.0 %copy-start = (bf16[8,8,128,128]{3,2,1,0:T(8,128)(2,1)S(1)}, bf16[8,8,128,128]{3,2,1,0:T(8,128)(2,1)}, u32[]{:S(2)}) copy-start(bf16[8,8,128,128]{3,2,1,0:T(8,128)(2,1)} %param.16) | copy-start | bytes 6291460
  20.0 6.1 %copy-start.4 = (s32[64,4]{0,1:T(4,128)S(1)}, s32[64,4]{0,1:T(4,128)}, u32[]{:S(2)}) copy-start(s32[64,4]{0,1:T(4,128)} %param.12) | copy-start | bytes 3076
  20.0 6.4 %copy-start.2 = (f32[8192]{0:T(1024)S(1)}, f32[8192]{0:T(1024)}, u32[]{:S(2)}) copy-start(f32[8192]{0:T(1024)} %param.14) | copy-start | bytes 98308
  21.6 30.8 %all-to-all-start = ((bf16[4,128,2048]{1,2,0:T(8,128)(2,1)}), bf16[4,128,2048]{1,2,0:T(8,128)(2,1)}, u32[]{:S(2)}, u32[]{:S(2)}) async-start(bf16[4,128,2048]{1,2,0:T(8,128)(2,1)} %pad_maximum_fusion), calls=%async_computation | async-start | bytes 4194304 | tf_op jit(solution)/shard_map/all_to_all | solution.py:42
  26.1 138.9 %reduce-scatter.2.cloned.1.call-start = ((), (), s32[]{:S(2)}) async-start(), calls=%async_computation.2 | async-start | bytes 2621440 | tf_op jit(solution)/shard_map/reduce_scatter | solution.py:56
  57.1 4.8 %copy-start.1 = (f32[8192]{0:T(1024)S(1)}, f32[8192]{0:T(1024)}, u32[]{:S(2)}) copy-start(f32[8192]{0:T(1024)} %param.13) | copy-start | bytes 98308
  73.8 46.0 %copy-start.3 = (s32[8,8]{1,0:T(8,128)S(1)}, s32[8,8]{1,0:T(8,128)}, u32[]{:S(2)}) copy-start(s32[8,8]{1,0:T(8,128)} %param.17) | copy-start | bytes 772
Sparse Core Ops, SparseCore 0:
  119.9 45.0 reduce-scatter.1
